TPU v7x, 512 devices: a whole 4x4x16 slice. The times are simulated.
512 devices in a mesh: row: 4 (over x), col: 16 (over z_lo, y), depth: 8 (over z_hi, core).
Axes of the slice: x: 4, y: 4, z: 16 (z_hi: 4, z_lo: 4; z = z_hi * 4 + z_lo), core: 2. Of those that a mesh axis runs over, the one named last changes fastest.
Arguments:
- amplitude: float32 [100, 512, 2048], P('row', 'depth', 'col'), may hold values from -6 to 6
- integral: float32 [512, 100, 8192], P('depth', None, 'col'), may hold values from -0.02734375 to 0.02734375
Outputs:
- cycle_term: float32 [2048, 8192], P(('row', 'depth'), 'col')
All inputs are finite; a program needn't handle non-finite values.
Results may differ from a plain program's by a relative error of at most 0.00011.
Values sent between devices are 32-bit elements; how exact they have to be, the bound alone decides.
A program may use at most 128 MiB of HBM per device.

v0:
```python
import jax
import jax.numpy as jnp
from jax import lax
from jax.sharding import PartitionSpec as P


def shards(amplitude, integral):
    remapped = lax.all_to_all(
        lax.all_to_all(amplitude, "col", split_axis=1, concat_axis=2, tiled=True),
        "row",
        split_axis=2,
        concat_axis=0,
        tiled=True,
    )
    product = jnp.einsum(
        "kcm,ckn->mn",
        lax.all_gather(remapped, "col", axis=1, tiled=True),
        integral,
        precision=lax.Precision.HIGHEST,
        preferred_element_type=jnp.float32,
    )
    return lax.psum_scatter(product, "depth", scatter_dimension=0, tiled=True)


def solution(mesh):
    return jax.shard_map(
        shards,
        mesh=mesh,
        in_specs=(P("row", "depth", "col"), P("depth", None, "col")),
        out_specs=P(("row", "depth"), "col"),
        check_vma=False,
    )
```

profile of v0, /device:TPU:14, one launch (start us, length us, event | category | flops | bytes accessed | tf_op | source)
XLA Modules:
  0.0 340.5 jit_solution(16741255330666027566)
XLA Ops:
  6.5 0.0 all-gather.2.cloned.1.call-start
  6.5 1.6 copy.13
  8.2 33.8 %all_to_all.36 = f32[25,64,128]{2,0,1:T(8,128)S(1)} all-to-all(f32[25,64,128]{2,0,1:T(8,128)S(1)} %copy.13), channel_id=1, replica_groups=mesh['row'=4,'col'=16,'depth'=8] {'col'}, dimensions={1} | all-to-all | bytes 1638400 | tf_op jit(solution)/shard_map/all_to_all | solution.py:9
  42.0 3.1 copy.14
  45.1 6.2 %reshape.1 = f32[4,1,51200]{2,1,0:T(1,128)S(1)} reshape(f32[2048,4,25]{2,1,0:T(4,128)} %bitcast.14) | data formatting | bytes 1638400
  51.3 13.2 %all_to_all.37 = f32[4,1,51200]{2,1,0:T(1,128)S(1)} all-to-all(f32[4,1,51200]{2,1,0:T(1,128)S(1)} %reshape.1), channel_id=1, replica_groups=mesh['row'=4,'col'=16,'depth'=8] {'row'}, dimensions={0} | all-to-all | bytes 1638400 | tf_op jit(solution)/shard_map/all_to_all | solution.py:8
  64.6 0.5 broadcast
  65.1 3.0 reduce
  68.1 8.0 %reshape.2 = f32[2048,4,25]{2,1,0:T(4,128)} reshape(f32[4,51200]{1,0:T(4,128)S(1)} %reduce) | data formatting | bytes 1638400
  76.1 3.6 %copy.16 = f32[4,25,4,512]{3,2,1,0:T(4,128)S(1)} copy(f32[4,25,4,512]{1,2,3,0:T(4,128)} %bitcast.15) | data formatting | bytes 1638400 | tf_op jit(solution)/shard_map/all_to_all | solution.py:8
  79.7 1.2 copy.17
  80.8 0.0 all-gather.2.cloned.1.call-update
  80.9 0.0 reduce-scatter.2.cloned.1.call-start
  80.9 158.1 %all-gather.2.cloned.1.call-done = f32[100,64,512]{2,0,1:T(8,128)} async-done(((f32[100,4,512]{2,0,1:T(8,128)}), f32[100,64,512]{2,0,1:T(8,128)}) %all-gather.2.cloned.1.call-update) | async-done | bytes 13107216 | tf_op jit(solution)/shard_map/all_gather | solution.py:17
  239.0 35.9 %fusion.2 = f32[512,512]{1,0:T(8,128)} fusion(f32[100,64,512]{2,0,1:T(8,128)} %all-gather.2.cloned.1.call-done, f32[64,100,512]{2,0,1:T(8,128)} %param.3), kind=kOutput, calls=%fused_computation.2 | convolution fusion | flops 20132659200 | bytes 27262976 | tf_op jit(solution)/shard_map/kcm,ckn->mn/dot_general | solution.py:15
  274.9 0.0 reduce-scatter.2.cloned.1.call-update
  274.9 58.7 %reduce-scatter.2.cloned.1.call-done = f32[64,512]{1,0:T(8,128)} async-done(((f32[512,512]{1,0:T(8,128)}), f32[64,512]{1,0:T(8,128)}) %reduce-scatter.2.cloned.1.call-update) | async-done | bytes 131088 | tf_op jit(solution)/shard_map/reduce_scatter | solution.py:22
Async XLA Ops:
  6.5 232.4 %all-gather.2.cloned.1.call-start = ((), (), s32[]{:S(2)}) async-start(), calls=%async_computation.3 | async-start | bytes 14483456 | tf_op jit(solution)/shard_map/all_gather | solution.py:17
  80.9 252.8 %reduce-scatter.2.cloned.1.call-start = ((), (), s32[]{:S(2)}) async-start(), calls=%async_computation.4 | async-start | bytes 1179648 | tf_op jit(solution)/shard_map/reduce_scatter | solution.py:22
Sparse Core Ops, SparseCore 0:
  81.0 157.9 all-gather.1
  275.0 58.5 reduce-scatter.1
where the time goes:
time: 341 us; the launch traced here: 340 us
  waiting for transfers between devices  217 us (64%)
  blocking collectives  47 us (14%)
  matrix products  35.9 us (11%)
  local copies, waits for them, and re-layouts  24.2 us (7%)
  between operations  13.4 us (4%)
    all_gather x1, waiting for transfers between devices, shards(): lax.all_gather(remapped, 'col', axis=1, tiled=True)  158 us
    reduce_scatter x1, waiting for transfers between devices, shards(): return lax.psum_scatter(product, 'depth', scatter_dimension=0, tiled=True)  58.7 us
    dot_general x1, matrix products, shards(): jnp.einsum('kcm,ckn->mn', lax.all_gather(remapped, 'col', axis=1, tiled=T...  35.9 us
    all_to_all x1, blocking collectives, shards(): lax.all_to_all(amplitude, 'col', split_axis=1, concat_axis=2, tiled=True)  33.8 us
    unnamed x3, local copies, waits for them, and re-layouts  15.8 us
    all_to_all x1, blocking collectives, shards(): lax.all_to_all(lax.all_to_all(amplitude, 'col', split_axis=1, concat_axis...  13.2 us
  transfers between devices with their start and end apart: 2, of which 2 were waited for; matrix products, arithmetic and copies ran while one was open for 0% of the time, Pallas kernels for 0%

commit v1 on v0

v1 whole, which is shorter than its diff:
```python
import functools

import jax
import jax.numpy as jnp
from jax import lax
from jax.experimental import pallas as pl
from jax.experimental.pallas import tpu as pltpu
from jax.sharding import PartitionSpec as P

MESH = pl.DeviceIdType.MESH
CH = 5
KC = 5
AHEAD = 3


def order(z, p):
    hi = z // 2
    zz = z + hi * (3 - 2 * z)
    base = p + zz * (1 - 2 * p) if p < 2 else p
    return base + hi * (3 - 2 * base)


def kernel(
    amp, integ, out,
    abuf, at_h, at_l, bown, bh, bl, ib, part, r1, r2, r3, fin,
    loc, zr, zd, zu, yr, ys, ir, js, s1s, s1r, s2s, s2r, s3s, s3r, s4s, s4r,
):
    x = lax.axis_index("row")
    col = lax.axis_index("col")
    dep = lax.axis_index("depth")
    z, y = col // 4, lax.rem(col, 4)
    h, core = dep // 2, lax.rem(dep, 2)
    yp = 3 - y
    yq = y + 1 - 2 * lax.rem(y, 2)
    ords = [order(z, p) for p in range(4)]

    def dev(x_=None, y_=None, z_=None, h_=None, core_=None):
        return (
            x if x_ is None else x_,
            (z if z_ is None else z_) * 4 + (y if y_ is None else y_),
            (h if h_ is None else h_) * 2 + (core if core_ is None else core_),
        )

    def remote(src, dst, ss, rs, to):
        return pltpu.make_async_remote_copy(
            src_ref=src, dst_ref=dst, send_sem=ss, recv_sem=rs,
            device_id=to, device_id_type=MESH,
        )

    own_a = pltpu.make_async_copy(amp, abuf.at[z], loc.at[0])
    own_b = pltpu.make_async_copy(integ.at[pl.ds(25 * x, 25)], bown, loc.at[1])
    own_a.start()
    own_b.start()

    barrier = pltpu.get_barrier_semaphore()

    def greet(to):
        pl.semaphore_signal(barrier, inc=1, device_id=to, device_id_type=MESH)

    greet(dev(y_=yp))
    greet(dev(y_=yq))
    greet(dev(core_=1 - core))
    for i in range(1, 4):
        greet(dev(x_=lax.rem(x + i, 4)))
        greet(dev(h_=lax.rem(h + i, 4)))

    @pl.when(z > 0)
    def _():
        greet(dev(z_=z - 1))

    @pl.when(z < 3)
    def _():
        greet(dev(z_=z + 1))

    @pl.when((z > 0) & (z < 3))
    def _():
        pl.semaphore_wait(barrier, 11)

    @pl.when((z == 0) | (z == 3))
    def _():
        pl.semaphore_wait(barrier, 10)

    own_a.wait()

    def int_copy(p, c):
        return remote(
            integ.at[pl.ds(25 * x + KC * c, KC), :, pl.ds(128 * p, 128)],
            ib.at[p, pl.ds(KC * c, KC)],
            js.at[p, c], ir.at[p, c], dev(y_=yq),
        )

    def y_copy(p, c):
        a = ords[p]
        ks = pl.ds(KC * c, KC)
        return remote(abuf.at[a, ks], abuf.at[4 + a, ks], ys.at[a, c], yr.at[a, c], dev(y_=yp))

    def z_copy(a, c, to, sem):
        ks = pl.ds(KC * c, KC)
        return remote(abuf.at[a, ks], abuf.at[a, ks], sem.at[a, c], zr.at[a, c], dev(z_=to))

    def feed(p, c, do_z):
        int_copy(p, c).start()
        y_copy(p, c).start()
        if p < 3:
            @pl.when((z > 0) & (z + p <= 3))
            def _():
                z_copy(z + p, c, z - 1, zd).start()

            @pl.when((z < 3) & (z - p >= 0))
            def _():
                z_copy(z - p, c, z + 1, zu).start()

    def arrive(p, c):
        int_copy(p, c).wait_recv()
        y_copy(p, c).wait_recv()
        if p < 3:
            @pl.when(z + p + 1 <= 3)
            def _():
                z_copy(z + p + 1, c, z - 1, zd).wait_recv()

            @pl.when(z - p - 1 >= 0)
            def _():
                z_copy(z - p - 1, c, z + 1, zu).wait_recv()

    def tick(t):
        arrive(t // CH, t % CH)
        if t + AHEAD < 4 * CH:
            feed((t + AHEAD) // CH, (t + AHEAD) % CH, True)

    def messages(p):
        got = []
        if p <= 3:
            got.append((0, p, True))
        if p >= 1:
            got.append((1, p - 1, True))
        for e in range(min(p, 4)):
            got.append((0, e, False))
        for e in range(p - 1):
            got.append((1, e, False))
        return got

    def cols_of(p, new):
        return (0, 512 + 128 * p) if new else (512 + 128 * (p - 1), 128)

    def slot_of(side, e):
        return 4 * side + ords[e]

    def split(v):
        hi = v.astype(jnp.bfloat16)
        return hi, (v - hi.astype(jnp.float32)).astype(jnp.bfloat16)

    def prep_a(slot):
        t = abuf[slot].reshape(1600, 128).T
        hi, lo = split(t)
        at_h[slot] = hi
        at_l[slot] = lo

    def multiply(slot, c0, width):
        ah = at_h[slot]
        al = at_l[slot]
        n0 = c0
        while n0 < c0 + width:
            w = min(256, c0 + width - n0)
            b_h = bh[:, n0:n0 + w]
            b_l = bl[:, n0:n0 + w]
            acc = jnp.dot(ah, b_l, preferred_element_type=jnp.float32)
            acc += jnp.dot(al, b_h, preferred_element_type=jnp.float32)
            acc += jnp.dot(ah, b_h, preferred_element_type=jnp.float32)
            part[slot, :, :, n0:n0 + w] = acc.reshape(2, 64, w)
            n0 += w

    def s1_copy(p, m):
        side, e, new = m
        slot = slot_of(side, e)
        c0, w = cols_of(p, new)
        cs = pl.ds(c0, w)
        return remote(
            part.at[slot, 1 - core, :, cs], r1.at[slot, :, cs],
            s1s.at[slot, p], s1r.at[slot, p], dev(core_=1 - core),
        )

    def s2_copy(p, m, src_x):
        side, e, new = m
        slot = slot_of(side, e)
        c0, w = cols_of(p, new)
        cs = pl.ds(c0, w)
        a = ords[e]
        i = lax.rem(src_x - a + 3, 4)
        return remote(
            part.at[slot, core, :, cs], r2.at[side, i, :, cs],
            s2s.at[slot, p], s2r.at[side, i, p], dev(x_=a),
        )

    def s3_copy(p, m, src_h):
        side, e, new = m
        slot = slot_of(side, e)
        c0, w = cols_of(p, new)
        cs = pl.ds(c0, w)
        b = yp if side else y
        i = lax.rem(src_h - b + 3, 4)
        return remote(
            part.at[slot, core, :, cs], r3.at[i, :, cs],
            s3s.at[side, p], s3r.at[i, p], dev(h_=b),
        )

    def s4_copy(p, m):
        side, e, new = m
        slot = slot_of(side, e)
        c0, w = cols_of(p, new)
        if new:
            c0, w = 512, w - 512
        return remote(
            part.at[slot, core, :, pl.ds(c0, w)], fin.at[:, pl.ds(c0 - 512, w)],
            s4s.at[p], s4r.at[p], dev(y_=yq),
        )

    def stage2(p):
        for m in messages(p):
            side, e, new = m
            slot = slot_of(side, e)
            c0, w = cols_of(p, new)
            s1_copy(p, m).wait_recv()
            part[slot, core, :, c0:c0 + w] = part[slot, core, :, c0:c0 + w] + r1[slot, :, c0:c0 + w]

            @pl.when(ords[e] != x)
            def _():
                s2_copy(p, m, x).start()

    def stage3(p):
        for m in messages(p):
            side, e, new = m
            slot = slot_of(side, e)
            c0, w = cols_of(p, new)
            b = yp if side else y

            @pl.when(ords[e] == x)
            def _():
                for i in range(3):
                    s2_copy(p, m, lax.rem(ords[e] + 1 + i, 4)).wait_recv()
                part[slot, core, :, c0:c0 + w] = (
                    part[slot, core, :, c0:c0 + w] + r2[side, 0, :, c0:c0 + w]
                ) + (r2[side, 1, :, c0:c0 + w] + r2[side, 2, :, c0:c0 + w])

                @pl.when(h != b)
                def _():
                    s3_copy(p, m, h).start()

    def stage4(p):
        for m in messages(p):
            side, e, new = m
            slot = slot_of(side, e)
            c0, w = cols_of(p, new)
            b = yp if side else y

            @pl.when((ords[e] == x) & (h == b))
            def _():
                for i in range(3):
                    s3_copy(p, m, lax.rem(b + 1 + i, 4)).wait_recv()
                total = (part[slot, core, :, c0:c0 + w] + r3[0, :, c0:c0 + w]) + (
                    r3[1, :, c0:c0 + w] + r3[2, :, c0:c0 + w]
                )
                if new:
                    out[...] = total[:, :512]
                    if p:
                        part[slot, core, :, 512:c0 + w] = total[:, 512:]
                else:
                    part[slot, core, :, c0:c0 + w] = total
                if p:
                    s4_copy(p, m).start()

    def compute_new(p):
        for m in messages(p):
            if m[2]:
                slot = slot_of(m[0], m[1])
                prep_a(slot)
                multiply(slot, *cols_of(p, True))
                s1_copy(p, m).start()

    def compute_old(p):
        for m in messages(p):
            if not m[2]:
                multiply(slot_of(m[0], m[1]), *cols_of(p, False))
                s1_copy(p, m).start()

    def prep_b_own():
        @pl.loop(0, 25)
        def _(k):
            hi, lo = split(bown[k])
            rows = pl.ds(pl.multiple_of(64 * k, 64), 64)
            bh[rows, 0:512] = hi
            bl[rows, 0:512] = lo

    def prep_b(q):
        @pl.loop(0, 25)
        def _(k):
            hi, lo = split(ib[q, k])
            rows = pl.ds(pl.multiple_of(64 * k, 64), 64)
            bh[rows, 512 + 128 * q:640 + 128 * q] = hi
            bl[rows, 512 + 128 * q:640 + 128 * q] = lo

    for t in range(AHEAD):
        feed(t // CH, t % CH, True)
    own_b.wait()
    tick(0)
    prep_b_own()
    tick(1)
    compute_new(0)
    tick(2)
    tick(3)
    tick(4)
    for p in range(1, 4):
        tick(CH * p)
        prep_b(p - 1)
        stage2(p - 1)
        compute_new(p)
        tick(CH * p + 1)
        tick(CH * p + 2)
        compute_old(p)
        tick(CH * p + 3)
        stage3(p - 1)
        if p >= 2:
            stage4(p - 2)
        tick(CH * p + 4)
    prep_b(3)
    stage2(3)
    compute_new(4)
    compute_old(4)
    stage4(2)
    stage3(3)
    stage2(4)
    stage3(4)
    stage4(3)
    stage4(4)

    for side in range(2):
        b = 3 - yq if side else yq
        for e in range(4):
            @pl.when((ords[e] == x) & (h == b))
            def _():
                first = e + side
                for p in range(max(first, 1), 5):
                    s4_copy(p, (side, e, p == first)).wait_recv()
                out[...] = fin[...]

    for p in range(4):
        for c in range(CH):
            int_copy(p, c).wait_send()
            y_copy(p, c).wait_send()
            if p < 3:
                @pl.when((z > 0) & (z + p <= 3))
                def _():
                    z_copy(z + p, c, z - 1, zd).wait_send()

                @pl.when((z < 3) & (z - p >= 0))
                def _():
                    z_copy(z - p, c, z + 1, zu).wait_send()
    for p in range(5):
        for m in messages(p):
            side, e, new = m
            b = yp if side else y
            s1_copy(p, m).wait_send()

            @pl.when(ords[e] != x)
            def _():
                s2_copy(p, m, x).wait_send()

            @pl.when((ords[e] == x) & (h != b))
            def _():
                s3_copy(p, m, h).wait_send()

            if p:
                @pl.when((ords[e] == x) & (h == b))
                def _():
                    s4_copy(p, m).wait_send()


def shards(amplitude, integral):
    f32, bf16 = jnp.float32, jnp.bfloat16
    dma = pltpu.SemaphoreType.DMA
    return pl.pallas_call(
        kernel,
        out_shape=jax.ShapeDtypeStruct((64, 512), f32),
        in_specs=[pl.BlockSpec(memory_space=pl.ANY)] * 2,
        out_specs=pl.BlockSpec(memory_space=pltpu.VMEM),
        scratch_shapes=[
            pltpu.VMEM((8, 25, 64, 128), f32),
            pltpu.VMEM((8, 128, 1600), bf16),
            pltpu.VMEM((8, 128, 1600), bf16),
            pltpu.VMEM((25, 64, 512), f32),
            pltpu.VMEM((1600, 1024), bf16),
            pltpu.VMEM((1600, 1024), bf16),
            pltpu.VMEM((4, 25, 64, 128), f32),
            pltpu.VMEM((8, 2, 64, 1024), f32),
            pltpu.VMEM((8, 64, 1024), f32),
            pltpu.VMEM((2, 3, 64, 1024), f32),
            pltpu.VMEM((3, 64, 1024), f32),
            pltpu.VMEM((64, 512), f32),
            dma((2,)),
            dma((4, CH)), dma((4, CH)), dma((4, CH)),
            dma((4, CH)), dma((4, CH)),
            dma((4, CH)), dma((4, CH)),
            dma((8, 5)), dma((8, 5)),
            dma((8, 5)), dma((2, 3, 5)),
            dma((2, 5)), dma((3, 5)),
            dma((5,)), dma((5,)),
        ],
        compiler_params=pltpu.CompilerParams(
            collective_id=0, has_side_effects=True, vmem_limit_bytes=56 << 20
        ),
    )(amplitude, jnp.transpose(integral, (1, 0, 2)))


def solution(mesh):
    return jax.shard_map(
        shards,
        mesh=mesh,
        in_specs=(P("row", "depth", "col"), P("depth", None, "col")),
        out_specs=P(("row", "depth"), "col"),
        check_vma=False,
    )
```

time: 341 us -> 144 us (0.42)
  the two profiles are of different devices: /device:TPU:14 before, /device:TPU:112 now
where the time goes in v1:
time: 144 us
  Pallas kernels  142 us (99%)
  local copies, waits for them, and re-layouts  1.57 us (1%)
    pallas_call x1, Pallas kernels, shards(): pl.pallas_call(kernel, out_shape=jax.ShapeDtypeStruct((64, 512), f32), in...  142 us

profile of v1, /device:TPU:112, one launch (start us, length us, event | category | flops | bytes accessed | tf_op | source)
XLA Modules:
  0.0 143.9 jit_solution(18280531657962536982)
XLA Ops:
  0.0 142.3 %shard_map.28 = f32[64,512]{1,0:T(8,128)} custom-call(f32[25,64,128]{2,1,0:T(8,128)} %amp.1, f32[100,64,512]{2,1,0:T(8,128)} %bitcast.1), custom_call_target="tpu_custom_call" | custom-call | tf_op jit(solution)/shard_map/pallas_call | solution.py:380
  142.3 1.6 %copy.4 = f32[64,512]{1,0:T(8,128)} copy(f32[64,512]{1,0:T(8,128)} %shard_map.28) | data formatting | bytes 262144

commit v2 on v1

v2 whole, which is shorter than its diff:
```python
import functools

import jax
import jax.numpy as jnp
from jax import lax
from jax.experimental import pallas as pl
from jax.experimental.pallas import tpu as pltpu
from jax.sharding import PartitionSpec as P

MESH = pl.DeviceIdType.MESH
CH = 5
KC = 5
AHEAD = 3


def order(z, p):
    hi = z // 2
    zz = z + hi * (3 - 2 * z)
    base = p + zz * (1 - 2 * p) if p < 2 else p
    return base + hi * (3 - 2 * base)


def kernel(
    amp, integ, out,
    abuf, at_h, at_l, bown, bh, bl, ib, part, r1, r2, r3, fin,
    loc, zr, zd, zu, yr, ys, ir, js, s1s, s1r, s2s, s2r, s3s, s3r, s4s, s4r,
):
    x = lax.axis_index("row")
    col = lax.axis_index("col")
    dep = lax.axis_index("depth")
    z, y = col // 4, lax.rem(col, 4)
    h, core = dep // 2, lax.rem(dep, 2)
    yp = 3 - y

    def flip(v):
        return v + 1 - 2 * lax.rem(v, 2)

    yq = flip(y)
    ords = [order(z, p) for p in range(4)]

    def dev(x_=None, y_=None, z_=None, h_=None, core_=None):
        return (
            x if x_ is None else x_,
            (z if z_ is None else z_) * 4 + (y if y_ is None else y_),
            (h if h_ is None else h_) * 2 + (core if core_ is None else core_),
        )

    def remote(src, dst, ss, rs, to):
        return pltpu.make_async_remote_copy(
            src_ref=src, dst_ref=dst, send_sem=ss, recv_sem=rs,
            device_id=to, device_id_type=MESH,
        )

    own_a = pltpu.make_async_copy(amp, abuf.at[z], loc.at[0])
    own_b = pltpu.make_async_copy(integ.at[pl.ds(25 * x, 25)], bown, loc.at[1])
    own_a.start()
    own_b.start()

    barrier = pltpu.get_barrier_semaphore()

    def greet(to):
        pl.semaphore_signal(barrier, inc=1, device_id=to, device_id_type=MESH)

    greet(dev(y_=yp))
    greet(dev(y_=yq))
    greet(dev(core_=1 - core))
    for i in range(1, 4):
        greet(dev(x_=lax.rem(x + i, 4)))
        greet(dev(h_=lax.rem(h + i, 4)))

    @pl.when(z > 0)
    def _():
        greet(dev(z_=z - 1))

    @pl.when(z < 3)
    def _():
        greet(dev(z_=z + 1))

    @pl.when((z > 0) & (z < 3))
    def _():
        pl.semaphore_wait(barrier, 11)

    @pl.when((z == 0) | (z == 3))
    def _():
        pl.semaphore_wait(barrier, 10)

    own_a.wait()

    def int_copy(p, c):
        return remote(
            integ.at[pl.ds(25 * x + KC * c, KC), :, pl.ds(128 * p, 128)],
            ib.at[p, pl.ds(KC * c, KC)],
            js.at[p, c], ir.at[p, c], dev(y_=yq),
        )

    def y_copy(p, c):
        a = ords[p]
        ks = pl.ds(KC * c, KC)
        return remote(abuf.at[a, ks], abuf.at[4 + a, ks], ys.at[a, c], yr.at[a, c], dev(y_=yp))

    def z_copy(a, c, to, sem):
        ks = pl.ds(KC * c, KC)
        return remote(abuf.at[a, ks], abuf.at[a, ks], sem.at[a, c], zr.at[a, c], dev(z_=to))

    def feed(p, c, do_z):
        int_copy(p, c).start()
        y_copy(p, c).start()
        if p < 3:
            @pl.when((z > 0) & (z + p <= 3))
            def _():
                z_copy(z + p, c, z - 1, zd).start()

            @pl.when((z < 3) & (z - p >= 0))
            def _():
                z_copy(z - p, c, z + 1, zu).start()

    def arrive(p, c):
        int_copy(p, c).wait_recv()
        y_copy(p, c).wait_recv()
        if p < 3:
            @pl.when(z + p + 1 <= 3)
            def _():
                z_copy(z + p + 1, c, z - 1, zd).wait_recv()

            @pl.when(z - p - 1 >= 0)
            def _():
                z_copy(z - p - 1, c, z + 1, zu).wait_recv()

    def drain(p, c):
        int_copy(p, c).wait_send()
        y_copy(p, c).wait_send()
        if p < 3:
            @pl.when((z > 0) & (z + p <= 3))
            def _():
                z_copy(z + p, c, z - 1, zd).wait_send()

            @pl.when((z < 3) & (z - p >= 0))
            def _():
                z_copy(z - p, c, z + 1, zu).wait_send()

    def tick(t):
        arrive(t // CH, t % CH)
        if t:
            drain((t - 1) // CH, (t - 1) % CH)
        if t + AHEAD < 4 * CH:
            feed((t + AHEAD) // CH, (t + AHEAD) % CH, True)

    def fresh(p):
        if p == 4:
            return [(1, 3, 0, 512, 4), (1, 3, 512, 512, 5)]
        got = [(0, p, 0, 512 + 128 * p, p)]
        if p:
            got.append((1, p - 1, 0, 512 + 128 * p, p))
        return got

    def older(p):
        c0 = 512 + 128 * (p - 1)
        got = [(0, e, c0, 128, p) for e in range(min(p, 4))]
        return got + [(1, e, c0, 128, p) for e in range(p - 1)]

    def messages(p):
        return fresh(p) + older(p)

    def slot_of(side, e):
        return 4 * side + ords[e]

    def split(v):
        hi = v.astype(jnp.bfloat16)
        return hi, (v - hi.astype(jnp.float32)).astype(jnp.bfloat16)

    def prep_a(slot):
        t = abuf[slot].reshape(1600, 128).T
        hi, lo = split(t)
        at_h[slot] = hi
        at_l[slot] = lo

    def multiply(slot, c0, width):
        ah = at_h[slot]
        al = at_l[slot]
        n0 = c0
        while n0 < c0 + width:
            w = min(256, c0 + width - n0)
            b_h = bh[:, n0:n0 + w]
            b_l = bl[:, n0:n0 + w]
            acc = jnp.dot(ah, b_l, preferred_element_type=jnp.float32)
            acc += jnp.dot(al, b_h, preferred_element_type=jnp.float32)
            acc += jnp.dot(ah, b_h, preferred_element_type=jnp.float32)
            part[slot, :, :, n0:n0 + w] = acc.reshape(2, 64, w)
            n0 += w

    def s1_copy(m):
        side, e, c0, w, q = m
        slot = slot_of(side, e)
        cs = pl.ds(c0, w)
        return remote(
            part.at[slot, 1 - core, :, cs], r1.at[slot, :, cs],
            s1s.at[slot, q], s1r.at[slot, q], dev(core_=1 - core),
        )

    def part_rows(slot, i, cs):
        return part.at[slot, core, pl.ds(pl.multiple_of(16 * i, 16), 16), cs]

    def s2_copy(m, i, src_x, to):
        side, e, c0, w, q = m
        slot = slot_of(side, e)
        cs = pl.ds(c0, w)
        return remote(
            part_rows(slot, to, cs), r2.at[slot, i, :, cs],
            s2s.at[slot, i, q], s2r.at[slot, i, q], dev(x_=to),
        )

    def s3_copy(m, i):
        side, e, c0, w, q = m
        slot = slot_of(side, e)
        cs = pl.ds(c0, w)
        b = yp if side else y
        to = flip(b) if i == 0 else b
        k = 1 if i == 1 else 0
        return remote(
            part_rows(slot, x, cs), r3.at[ords[e], k, :, cs],
            s3s.at[slot, q], s3r.at[ords[e], k, q], dev(h_=to),
        )

    def fin_rows(i, cs):
        return fin.at[pl.ds(pl.multiple_of(16 * i, 16), 16), cs]

    def s4_own(side, e, src_x):
        slot = slot_of(side, e)
        cs = pl.ds(0, 512)
        return remote(
            part_rows(slot, x, cs), fin_rows(src_x, cs),
            s4s.at[ords[e], 0], s4r.at[src_x, 0], dev(x_=ords[e]),
        )

    def s4_far(m, src_x):
        side, e, c0, w, q = m
        slot = slot_of(side, e)
        w, c0 = c0 + w - max(c0, 512), max(c0, 512)
        return remote(
            part_rows(slot, x, pl.ds(c0, w)), fin_rows(src_x, pl.ds(c0 - 512, w)),
            s4s.at[ords[e], q], s4r.at[src_x, q], dev(x_=ords[e], y_=yq),
        )

    def stage2(p, pick=None):
        for m in messages(p) if pick is None else pick:
            side, e, c0, w, q = m
            slot = slot_of(side, e)
            s1_copy(m).wait_recv()
            part[slot, core, :, c0:c0 + w] = part[slot, core, :, c0:c0 + w] + r1[slot, :, c0:c0 + w]
            for i in range(3):
                s2_copy(m, i, x, lax.rem(x + 1 + i, 4)).start()

    def stage3(p, pick=None):
        for m in messages(p) if pick is None else pick:
            side, e, c0, w, q = m
            slot = slot_of(side, e)
            b = yp if side else y
            for i in range(3):
                s2_copy(m, i, x, lax.rem(x + 1 + i, 4)).wait_recv()
            rows = pl.ds(pl.multiple_of(16 * x, 16), 16)
            part[slot, core, rows, c0:c0 + w] = (
                part[slot, core, rows, c0:c0 + w] + r2[slot, 0, :, c0:c0 + w]
            ) + (r2[slot, 1, :, c0:c0 + w] + r2[slot, 2, :, c0:c0 + w])

            @pl.when(h == lax.rem(b + 2, 4))
            def _():
                s3_copy(m, 0).start()

            @pl.when(h == 3 - b)
            def _():
                s3_copy(m, 1).start()

    def stage3m(p, pick=None):
        for m in messages(p) if pick is None else pick:
            side, e, c0, w, q = m
            slot = slot_of(side, e)
            b = yp if side else y

            @pl.when(h == flip(b))
            def _():
                s3_copy(m, 0).wait_recv()
                rows = pl.ds(pl.multiple_of(16 * x, 16), 16)
                part[slot, core, rows, c0:c0 + w] = (
                    part[slot, core, rows, c0:c0 + w] + r3[ords[e], 0, :, c0:c0 + w]
                )
                s3_copy(m, 2).start()

    def stage4(p, pick=None):
        for m in messages(p) if pick is None else pick:
            side, e, c0, w, q = m
            slot = slot_of(side, e)
            b = yp if side else y
            a = ords[e]

            @pl.when(h == b)
            def _():
                s3_copy(m, 1).wait_recv()
                s3_copy(m, 2).wait_recv()
                rows = pl.ds(pl.multiple_of(16 * x, 16), 16)
                part[slot, core, rows, c0:c0 + w] = part[slot, core, rows, c0:c0 + w] + (
                    r3[a, 0, :, c0:c0 + w] + r3[a, 1, :, c0:c0 + w]
                )
                if c0 + w > 512:
                    s4_far(m, x).start()
                if c0 == 0:
                    @pl.when(a == x)
                    def _():
                        fin[rows, :] = part[slot, core, rows, 0:512]

                    @pl.when(a != x)
                    def _():
                        s4_own(side, e, x).start()

    def sent(p):
        for m in messages(p):
            s1_copy(m).wait_send()
            for i in range(3):
                s2_copy(m, i, x, lax.rem(x + 1 + i, 4)).wait_send()

    def compute_new(p):
        for m in fresh(p):
            side, e, c0, w, q = m
            slot = slot_of(side, e)
            if c0 == 0:
                prep_a(slot)
            multiply(slot, c0, w)
            s1_copy(m).start()

    def compute_old(ms):
        for m in ms:
            side, e, c0, w, q = m
            multiply(slot_of(side, e), c0, w)
            s1_copy(m).start()

    def prep_b_own():
        @pl.loop(0, 25)
        def _(k):
            hi, lo = split(bown[k])
            rows = pl.ds(pl.multiple_of(64 * k, 64), 64)
            bh[rows, 0:512] = hi
            bl[rows, 0:512] = lo

    def prep_b(q):
        @pl.loop(0, 25)
        def _(k):
            hi, lo = split(ib[q, k])
            rows = pl.ds(pl.multiple_of(64 * k, 64), 64)
            bh[rows, 512 + 128 * q:640 + 128 * q] = hi
            bl[rows, 512 + 128 * q:640 + 128 * q] = lo

    for t in range(AHEAD):
        feed(t // CH, t % CH, True)
    own_b.wait()
    tick(0)
    prep_b_own()
    tick(1)
    compute_new(0)
    tick(2)
    tick(3)
    stage2(0)
    tick(4)
    tick(5)
    prep_b(0)
    compute_new(1)
    tick(6)
    compute_old(older(1))
    tick(7)
    stage2(1)
    tick(8)
    tick(9)
    tick(10)
    prep_b(1)
    compute_new(2)
    tick(11)
    stage3(0)
    stage3(1)
    compute_old(older(2))
    tick(12)
    stage2(2)
    tick(13)
    stage3m(0)
    stage3m(1)
    sent(0)
    sent(1)
    tick(14)
    tick(15)
    prep_b(2)
    stage3(2)
    compute_new(3)
    tick(16)
    stage2(3, fresh(3))
    compute_old(older(3))
    tick(17)
    stage2(3, older(3))
    stage3m(2)
    tick(18)
    stage3(3, fresh(3))
    stage4(0)
    stage4(1)
    sent(2)
    tick(19)
    prep_b(3)
    compute_new(4)
    stage3(3, older(3))
    compute_old(older(4)[:3])
    stage2(4, fresh(4))
    stage3m(3)
    compute_old(older(4)[3:])
    stage4(2)
    stage3(4, fresh(4))
    stage2(4, older(4))
    sent(3)
    stage3m(4, fresh(4))
    stage3(4, older(4))
    stage4(3)
    stage4(4, fresh(4))
    stage3m(4, older(4))
    sent(4)
    stage4(4, older(4))

    for side in range(2):
        for e in range(4):
            @pl.when((ords[e] == x) & (h == (yp if side else y)))
            def _():
                for i in range(3):
                    s4_own(side, e, lax.rem(x + 1 + i, 4)).wait_recv()

            @pl.when((ords[e] == x) & (h == (3 - yq if side else yq)))
            def _():
                for p in range(5):
                    for m in messages(p):
                        if m[:2] == (side, e) and m[2] + m[3] > 512:
                            for i in range(4):
                                s4_far(m, i).wait_recv()
    out[...] = fin[...]

    drain(3, CH - 1)
    for p in range(5):
        for m in messages(p):
            side, e, c0, w, q = m
            b = yp if side else y

            @pl.when(h != b)
            def _():
                s3_copy(m, 1).wait_send()

            @pl.when(h == b)
            def _():
                if c0 + w > 512:
                    s4_far(m, x).wait_send()
                if c0 == 0:
                    @pl.when(ords[e] != x)
                    def _():
                        s4_own(side, e, x).wait_send()


def shards(amplitude, integral):
    f32, bf16 = jnp.float32, jnp.bfloat16
    dma = pltpu.SemaphoreType.DMA
    return pl.pallas_call(
        kernel,
        out_shape=jax.ShapeDtypeStruct((64, 512), f32),
        in_specs=[pl.BlockSpec(memory_space=pl.ANY)] * 2,
        out_specs=pl.BlockSpec(memory_space=pltpu.VMEM),
        scratch_shapes=[
            pltpu.VMEM((8, 25, 64, 128), f32),
            pltpu.VMEM((8, 128, 1600), bf16),
            pltpu.VMEM((8, 128, 1600), bf16),
            pltpu.VMEM((25, 64, 512), f32),
            pltpu.VMEM((1600, 1024), bf16),
            pltpu.VMEM((1600, 1024), bf16),
            pltpu.VMEM((4, 25, 64, 128), f32),
            pltpu.VMEM((8, 2, 64, 1024), f32),
            pltpu.VMEM((8, 64, 1024), f32),
            pltpu.VMEM((8, 3, 16, 1024), f32),
            pltpu.VMEM((4, 2, 16, 1024), f32),
            pltpu.VMEM((64, 512), f32),
            dma((2,)),
            dma((4, CH)), dma((4, CH)), dma((4, CH)),
            dma((4, CH)), dma((4, CH)),
            dma((4, CH)), dma((4, CH)),
            dma((8, 6)), dma((8, 6)),
            dma((8, 3, 6)), dma((8, 3, 6)),
            dma((8, 6)), dma((4, 2, 6)),
            dma((4, 6)), dma((4, 6)),
        ],
        compiler_params=pltpu.CompilerParams(
            collective_id=0, has_side_effects=True, vmem_limit_bytes=56 << 20
        ),
    )(amplitude, jnp.transpose(integral, (1, 0, 2)))


def solution(mesh):
    return jax.shard_map(
        shards,
        mesh=mesh,
        in_specs=(P("row", "depth", "col"), P("depth", None, "col")),
        out_specs=P(("row", "depth"), "col"),
        check_vma=False,
    )
```

time: 144 us -> 124 us (0.86)
  the two profiles are of different devices: /device:TPU:112 before, /device:TPU:16 now
where the time goes in v2:
time: 124 us
  Pallas kernels  123 us (99%)
  local copies, waits for them, and re-layouts  1.57 us (1%)
    pallas_call x1, Pallas kernels, shards(): pl.pallas_call(kernel, out_shape=jax.ShapeDtypeStruct((64, 512), f32), in...  123 us

profile of v2, /device:TPU:16, one launch (start us, length us, event | category | flops | bytes accessed | tf_op | source)
XLA Modules:
  0.0 124.3 jit_solution(8820799349223473220)
XLA Ops:
  0.0 122.7 %shard_map.28 = f32[64,512]{1,0:T(8,128)} custom-call(f32[25,64,128]{2,1,0:T(8,128)} %amp.1, f32[100,64,512]{2,1,0:T(8,128)} %bitcast.1), custom_call_target="tpu_custom_call" | custom-call | tf_op jit(solution)/shard_map/pallas_call | solution.py:460
  122.7 1.6 %copy.4 = f32[64,512]{1,0:T(8,128)} copy(f32[64,512]{1,0:T(8,128)} %shard_map.28) | data formatting | bytes 262144

commit v3 on v2

--- a/solution.py
+++ b/solution.py
@@ -10,7 +10,7 @@
 MESH = pl.DeviceIdType.MESH
 CH = 5
 KC = 5
-AHEAD = 3
+AHEAD = 5
 
 
 def order(z, p):
@@ -23,7 +23,7 @@
 def kernel(
     amp, integ, out,
     abuf, at_h, at_l, bown, bh, bl, ib, part, r1, r2, r3, fin,
-    loc, zr, zd, zu, yr, ys, ir, js, s1s, s1r, s2s, s2r, s3s, s3r, s4s, s4r,
+    loc, ts, tr, zr, zd, zu, yr, ys, ir, js, s1s, s1r, s2s, s2r, s3s, s3r, s4s, s4r,
 ):
     x = lax.axis_index("row")
     col = lax.axis_index("col")
@@ -66,7 +66,8 @@
     greet(dev(core_=1 - core))
     for i in range(1, 4):
         greet(dev(x_=lax.rem(x + i, 4)))
-        greet(dev(h_=lax.rem(h + i, 4)))
+    greet(dev(h_=lax.rem(h + 1, 4)))
+    greet(dev(h_=lax.rem(h + 3, 4)))
 
     @pl.when(z > 0)
     def _():
@@ -78,11 +79,11 @@
 
     @pl.when((z > 0) & (z < 3))
     def _():
-        pl.semaphore_wait(barrier, 11)
+        pl.semaphore_wait(barrier, 10)
 
     @pl.when((z == 0) | (z == 3))
     def _():
-        pl.semaphore_wait(barrier, 10)
+        pl.semaphore_wait(barrier, 9)
 
     own_a.wait()
 
@@ -147,13 +148,15 @@
 
     def fresh(p):
         if p == 4:
-            return [(1, 3, 0, 512, 4), (1, 3, 512, 512, 5)]
+            return [(1, 3, 0, 512, 4), (1, 3, 512, 384, 5)]
         got = [(0, p, 0, 512 + 128 * p, p)]
         if p:
             got.append((1, p - 1, 0, 512 + 128 * p, p))
         return got
 
     def older(p):
+        if p == 4:
+            return []
         c0 = 512 + 128 * (p - 1)
         got = [(0, e, c0, 128, p) for e in range(min(p, 4))]
         return got + [(1, e, c0, 128, p) for e in range(p - 1)]
@@ -347,6 +350,122 @@
             rows = pl.ds(pl.multiple_of(64 * k, 64), 64)
             bh[rows, 512 + 128 * q:640 + 128 * q] = hi
             bl[rows, 512 + 128 * q:640 + 128 * q] = lo
+
+    LAST = 896
+    TAIL = pl.ds(LAST, 128)
+    PARTS = ((0, 10), (10, 20), (20, 25))
+
+    def multiply_part(slot, c0, width, k0, k1):
+        ah = at_h[slot, :, 64 * k0:64 * k1]
+        al = at_l[slot, :, 64 * k0:64 * k1]
+        n0 = c0
+        while n0 < c0 + width:
+            w = min(256, c0 + width - n0)
+            b_h = bh[64 * k0:64 * k1, n0:n0 + w]
+            b_l = bl[64 * k0:64 * k1, n0:n0 + w]
+            acc = jnp.dot(ah, b_l, preferred_element_type=jnp.float32)
+            acc += jnp.dot(al, b_h, preferred_element_type=jnp.float32)
+            acc += jnp.dot(ah, b_h, preferred_element_type=jnp.float32)
+            acc = acc.reshape(2, 64, w)
+            if k0:
+                acc += part[slot, :, :, n0:n0 + w]
+            part[slot, :, :, n0:n0 + w] = acc
+            n0 += w
+
+    def last_part(i):
+        k0, k1 = PARTS[i]
+        slot = slot_of(1, 3)
+        hi, lo = split(abuf[slot, k0:k1].reshape(64 * (k1 - k0), 128).T)
+        at_h[slot, :, 64 * k0:64 * k1] = hi
+        at_l[slot, :, 64 * k0:64 * k1] = lo
+        hi, lo = split(ib[3, k0:k1].reshape(64 * (k1 - k0), 128))
+        bh[64 * k0:64 * k1, LAST:1024] = hi
+        bl[64 * k0:64 * k1, LAST:1024] = lo
+        for m in fresh(4):
+            multiply_part(slot, m[2], m[3], k0, k1)
+            if i == 2:
+                s1_copy(m).start()
+
+        @pl.loop(0, 8)
+        def _(t):
+            multiply_part(t, LAST, 128, k0, k1)
+
+        if i == 2:
+            t1_copy().start()
+
+    def t1_copy():
+        return remote(
+            part.at[:, 1 - core, :, TAIL], r1.at[:, :, TAIL], ts.at[0], tr.at[0], dev(core_=1 - core)
+        )
+
+    def t2_copy(i):
+        to = lax.rem(x + 1 + i, 4)
+        rows = pl.ds(pl.multiple_of(16 * to, 16), 16)
+        return remote(
+            part.at[:, core, rows, TAIL], r2.at[:, i, :, TAIL], ts.at[1 + i], tr.at[1 + i], dev(x_=to)
+        )
+
+    def t3_copy(side, i):
+        b = yp if side else y
+        to = flip(b) if i == 0 else b
+        k = 1 if i == 1 else 0
+        rows = pl.ds(pl.multiple_of(16 * x, 16), 16)
+        return remote(
+            part.at[pl.ds(4 * side, 4), core, rows, TAIL], r3.at[:, k, :, TAIL],
+            ts.at[4 + side], tr.at[4 + k], dev(h_=to),
+        )
+
+    def tail2():
+        t1_copy().wait_recv()
+        for t in range(8):
+            part[t, core, :, LAST:1024] = part[t, core, :, LAST:1024] + r1[t, :, LAST:1024]
+        for i in range(3):
+            t2_copy(i).start()
+
+    def tail3():
+        for i in range(3):
+            t2_copy(i).wait_recv()
+        rows = pl.ds(pl.multiple_of(16 * x, 16), 16)
+        for t in range(8):
+            part[t, core, rows, LAST:1024] = (
+                part[t, core, rows, LAST:1024] + r2[t, 0, :, LAST:1024]
+            ) + (r2[t, 1, :, LAST:1024] + r2[t, 2, :, LAST:1024])
+        for side in range(2):
+            b = yp if side else y
+
+            @pl.when(h == lax.rem(b + 2, 4))
+            def _():
+                t3_copy(side, 0).start()
+
+            @pl.when(h == 3 - b)
+            def _():
+                t3_copy(side, 1).start()
+
+    def tail3m():
+        rows = pl.ds(pl.multiple_of(16 * x, 16), 16)
+        for side in range(2):
+            @pl.when(h == flip(yp if side else y))
+            def _():
+                t3_copy(side, 0).wait_recv()
+                for a in range(4):
+                    t = 4 * side + a
+                    part[t, core, rows, LAST:1024] = part[t, core, rows, LAST:1024] + r3[a, 0, :, LAST:1024]
+                t3_copy(side, 2).start()
+
+    def tail4():
+        rows = pl.ds(pl.multiple_of(16 * x, 16), 16)
+        for side in range(2):
+            @pl.when(h == (yp if side else y))
+            def _():
+                t3_copy(side, 1).wait_recv()
+                t3_copy(side, 2).wait_recv()
+                for a in range(4):
+                    t = 4 * side + a
+                    part[t, core, rows, LAST:1024] = part[t, core, rows, LAST:1024] + (
+                        r3[a, 0, :, LAST:1024] + r3[a, 1, :, LAST:1024]
+                    )
+                for e in range(4):
+                    s4_far((side, e, LAST, 128, 4), x).start()
 
     for t in range(AHEAD):
         feed(t // CH, t % CH, True)
@@ -390,33 +509,32 @@
     tick(16)
     stage2(3, fresh(3))
     compute_old(older(3))
+    last_part(0)
     tick(17)
     stage2(3, older(3))
     stage3m(2)
     tick(18)
     stage3(3, fresh(3))
+    last_part(1)
     stage4(0)
     stage4(1)
     sent(2)
     tick(19)
-    prep_b(3)
-    compute_new(4)
+    last_part(2)
     stage3(3, older(3))
-    compute_old(older(4)[:3])
-    stage2(4, fresh(4))
-    stage3m(3)
-    compute_old(older(4)[3:])
+    stage2(4)
+    stage3m(3, fresh(3))
+    tail2()
+    stage3(4)
+    stage3m(3, older(3))
     stage4(2)
-    stage3(4, fresh(4))
-    stage2(4, older(4))
+    tail3()
     sent(3)
-    stage3m(4, fresh(4))
-    stage3(4, older(4))
+    stage3m(4)
     stage4(3)
-    stage4(4, fresh(4))
-    stage3m(4, older(4))
-    sent(4)
-    stage4(4, older(4))
+    tail3m()
+    stage4(4)
+    tail4()
 
     for side in range(2):
         for e in range(4):
@@ -432,9 +550,27 @@
                         if m[:2] == (side, e) and m[2] + m[3] > 512:
                             for i in range(4):
                                 s4_far(m, i).wait_recv()
+                for i in range(4):
+                    s4_far((side, e, LAST, 128, 4), i).wait_recv()
     out[...] = fin[...]
 
     drain(3, CH - 1)
+    sent(4)
+    t1_copy().wait_send()
+    for i in range(3):
+        t2_copy(i).wait_send()
+    for side in range(2):
+        b = yp if side else y
+
+        @pl.when(h != b)
+        def _():
+            t3_copy(side, 1).wait_send()
+
+        @pl.when(h == b)
+        def _():
+            for e in range(4):
+                s4_far((side, e, LAST, 128, 4), x).wait_send()
+
     for p in range(5):
         for m in messages(p):
             side, e, c0, w, q = m
@@ -475,7 +611,7 @@
             pltpu.VMEM((8, 3, 16, 1024), f32),
             pltpu.VMEM((4, 2, 16, 1024), f32),
             pltpu.VMEM((64, 512), f32),
-            dma((2,)),
+            dma((2,)), dma((6,)), dma((6,)),
             dma((4, CH)), dma((4, CH)), dma((4, CH)),
             dma((4, CH)), dma((4, CH)),
             dma((4, CH)), dma((4, CH)),

time: 124 us -> 123 us (level)
  Pallas kernels: 123 us -> 121 us
    pallas_call x1, Pallas kernels: 123 us -> 121 us  [shards(): pl.pallas_call(kernel, out_shape=jax.ShapeDtypeStruct((64, 512), f32), in...]
where the time goes in v3:
time: 123 us
  Pallas kernels  121 us (98%)
  local copies, waits for them, and re-layouts  1.57 us (1%)
    pallas_call x1, Pallas kernels, shards(): pl.pallas_call(kernel, out_shape=jax.ShapeDtypeStruct((64, 512), f32), in...  121 us

profile of v3, /device:TPU:16, one launch (start us, length us, event | category | flops | bytes accessed | tf_op | source)
XLA Modules:
  0.0 122.9 jit_solution(10111486415008503159)
XLA Ops:
  0.0 121.3 %shard_map.28 = f32[64,512]{1,0:T(8,128)} custom-call(f32[25,64,128]{2,1,0:T(8,128)} %amp.1, f32[100,64,512]{2,1,0:T(8,128)} %bitcast.1), custom_call_target="tpu_custom_call" | custom-call | tf_op jit(solution)/shard_map/pallas_call | solution.py:596
  121.4 1.6 %copy.4 = f32[64,512]{1,0:T(8,128)} copy(f32[64,512]{1,0:T(8,128)} %shard_map.28) | data formatting | bytes 262144
